TPU v7x, 128 devices: a whole 4x4x4 slice. The times are simulated.
128 devices in a mesh: row: 8 (over x, z_lo), col: 16 (over y, z_hi, core).
Axes of the slice: x: 4, y: 4, z: 4 (z_hi: 2, z_lo: 2; z = z_hi * 2 + z_lo), core: 2. Of those that a mesh axis runs over, the one named last changes fastest.
Arguments:
- momentum: bfloat16 [16384, 16384], P('row', 'col'), may hold values from -6 to 6
- gradient: bfloat16 [16384, 16384], P('row', 'col'), may hold values from -43 to 43
- right_prev: float32 [16384, 512], P('col'), may hold values from -6 to 6
- weight: bfloat16 [16384, 16384], P('col', 'row'), may hold values from -0.046875 to 0.046875
- tokens: bfloat16 [256, 16384], P(None, 'row'), may hold values from -6 to 6
Outputs:
- new_momentum: bfloat16 [16384, 16384], P('row', 'col')
- new_basis: float32 [16384, 512], P('col')
- new_weight: bfloat16 [16384, 16384], P('col', 'row')
- projected: bfloat16 [256, 16384], P('row', 'col')
All inputs are finite; a program needn't handle non-finite values.
Results may differ from a plain program's by a relative error of at most 0.006.
Values may be sent and summed in bfloat16 or wider, within the bound.
No kernel may reach another device: no remote copies, remote signals or barrier semaphores. Data moves between devices by JAX's collectives and lax.ppermute only.
A program may use at most 128 MiB of HBM per device.

v0:
```python
import functools
import jax
import jax.numpy as jnp
from jax import lax
from jax.sharding import Mesh
from jax.sharding import PartitionSpec as P

DIN = 16384
COL = ("col_0", "col_1", "col_2")
ROW = ("row_0", "row_1")
ROW_COL = ("row_0", "row_1", "col_0", "col_1", "col_2")
decay_part = 0.05
step_size = 0.01
epsilon = 1e-06


def cut_along(array, dim, length):
    shape = array.shape
    pieces = array.reshape(*shape[:dim], length, shape[dim] // length, *shape[dim + 1 :])
    return jnp.moveaxis(pieces, dim, 0)


def summed_on_arrival(array, axis, dim):
    length = lax.axis_size(axis)
    pieces = lax.all_to_all(cut_along(array, dim, length), axis, 0, 0, tiled=True)
    return jnp.sum(pieces, axis=0)


def over_axes(array, axes):
    return functools.reduce(lax.psum, axes, array)


def joined_along(pieces, dim):
    pieces = jnp.moveaxis(pieces, 0, dim)
    shape = pieces.shape
    return pieces.reshape(*shape[:dim], shape[dim] * shape[dim + 1], *shape[dim + 2 :])


def from_everyone(array, axis):
    length = lax.axis_size(axis)
    return lax.all_to_all(
        jnp.broadcast_to(array[None], (length, *array.shape)), axis, 0, 0, tiled=True
    )


def collect(array, axis, dim):
    return joined_along(from_everyone(array, axis), dim)


def filled_up(lines, length):
    spare = -len(lines) % length
    return jnp.pad(lines, [(0, spare)] + [(0, 0)] * (lines.ndim - 1))


def spread(array, axis, root):
    lines = jnp.where(lax.axis_index(axis) == root, array, jnp.zeros_like(array)).reshape(
        -1, *array.shape[1:][-1:]
    )
    padded = filled_up(lines, lax.axis_size(axis))
    own = lax.psum_scatter(padded, axis, scatter_dimension=0, tiled=True)
    return lax.all_gather(own, axis, axis=0, tiled=True)[: len(lines)].reshape(array.shape)


def from_root(array, axis, root):
    return lax.dynamic_index_in_dim(lax.all_gather(array, axis), root, 0, keepdims=False)


def contract_first(lhs, rhs, highest):
    return lax.dot_general(
        lhs, rhs, (((0,), (0,)), ((), ())), precision=highest, preferred_element_type=jnp.float32
    )


def contract_last(lhs, rhs, highest):
    return lax.dot_general(
        lhs, rhs, (((1,), (1,)), ((), ())), precision=highest, preferred_element_type=jnp.float32
    )


def per_device(momentum, gradient, right_prev, weight, tokens):
    highest = lax.Precision.HIGHEST
    mixed = momentum.astype(jnp.float32) + gradient.astype(jnp.float32)
    partial_left = jnp.dot(mixed, right_prev, precision=highest, preferred_element_type=jnp.float32)
    left_raw = lax.psum(partial_left, COL)
    gram_matrix = lax.psum(contract_first(left_raw, left_raw, highest), ROW)
    factor = jnp.linalg.cholesky(gram_matrix)
    left_factor = lax.linalg.triangular_solve(
        factor, left_raw, left_side=False, lower=True, transpose_a=True
    )
    partial_right = contract_first(mixed, left_factor, highest)
    right_shard = summed_on_arrival(partial_right, ROW, 0)
    squares = over_axes(jnp.sum(right_shard * right_shard, axis=0), ROW_COL)
    right_factor = collect(right_shard, ROW, 0)
    new_basis = right_factor * lax.rsqrt(squares / DIN + epsilon)
    outer = contract_last(left_factor, right_factor, highest)
    new_momentum = (mixed - decay_part * outer).astype(jnp.bfloat16)
    span_count = lax.axis_size(COL) // lax.axis_size(ROW)
    col_index = lax.axis_index(COL)
    row_index = lax.axis_index(ROW)
    block_rows = left_factor.shape[0] // span_count
    own_block = lax.dynamic_slice_in_dim(
        left_factor, col_index % span_count * block_rows, block_rows, 0
    )
    left_tile = spread(own_block.astype(jnp.bfloat16), ROW, col_index // span_count)
    basis_send = new_basis.astype(jnp.bfloat16)
    pieces = [
        from_root(basis_send, COL, row_index * span_count + piece_index)
        for piece_index in range(span_count)
    ]
    basis_tile = jnp.concatenate(pieces, axis=0)
    update = lax.dot_general(
        left_tile, basis_tile, (((1,), (1,)), ((), ())), preferred_element_type=jnp.float32
    )
    new_weight = (weight.astype(jnp.float32) - step_size * update).astype(jnp.bfloat16)
    projected = summed_on_arrival(
        lax.dot_general(
            tokens, new_weight, (((1,), (1,)), ((), ())), preferred_element_type=jnp.float32
        ),
        ROW,
        0,
    ).astype(jnp.bfloat16)
    return (new_momentum, new_basis, new_weight, projected)


def solution(mesh):
    torus = Mesh(mesh.devices.reshape(4, 2, 4, 2, 2), ("row_0", "row_1", "col_0", "col_1", "col_2"))
    placed = (P(ROW, COL), P(ROW, COL), P(COL, None), P(COL, ROW), P(None, ROW))
    return jax.shard_map(
        per_device,
        mesh=torus,
        in_specs=placed,
        out_specs=(P(ROW, COL), P(COL, None), P(COL, ROW), P(ROW, COL)),
        check_vma=False,
    )
```

profile of v0, /device:TPU:10, one launch (start us, length us, event | category | flops | bytes accessed | tf_op | source)
XLA Modules:
  0.0 747.0 jit_solution(4212846563401317149)
XLA Ops:
  7.2 1.5 copy-done
  8.8 17.3 %fusion.1 = f32[2048,512]{1,0:T(8,128)} fusion(f32[1024,512]{1,0:T(8,128)S(1)} %copy-done, bf16[2048,1024]{1,0:T(8,128)(2,1)} %param.6, bf16[2048,1024]{1,0:T(8,128)(2,1)} %param.5), kind=kOutput, calls=%fused_computation.6 | convolution fusion | flops 12891193344 | bytes 14680064 | tf_op jit(solution)/shard_map/dot_general | solution.py:83
  26.2 147.3 %all-reduce.4.cloned.1.call-done = f32[2048,512]{1,0:T(8,128)} async-done(((f32[2048,512]{1,0:T(8,128)}), f32[2048,512]{1,0:T(8,128)}) %all-reduce.4.cloned.1.call-update) | async-done | bytes 4194320 | tf_op jit(solution)/shard_map/psum | solution.py:84
  173.5 11.6 %fusion.43 = f32[512,512]{0,1:T(8,128)} fusion(f32[2048,512]{1,0:T(8,128)} %all-reduce.4.cloned.1.call-done), kind=kOutput, calls=%fused_computation.86 | convolution fusion | flops 6442450944 | bytes 5242880 | tf_op jit(solution)/shard_map/dot_general | solution.py:69
  185.1 83.7 %all-reduce.6.cloned.1.call-done = f32[512,512]{0,1:T(8,128)} async-done(((f32[512,512]{0,1:T(8,128)}), f32[512,512]{0,1:T(8,128)}) %all-reduce.6.cloned.1.call-update) | async-done | bytes 1048592 | tf_op jit(solution)/shard_map/psum | solution.py:85
  268.8 1.6 copy.12
  270.4 1.4 fusion.21
  271.9 11.7 %cholesky.104 = f32[128,128]{1,0:T(8,128)S(1)} custom-call(f32[128,128]{1,0:T(8,128)S(1)} %cholesky.266), custom_call_target="Cholesky" | custom-call | tf_op jit(solution)/shard_map/jit(cholesky)/cholesky | solution.py:86
  283.6 9.8 %custom-call.30 = f32[1,128,128]{1,2,0:T(8,128)S(1)} custom-call(f32[1,128,128]{2,1,0:T(8,128)S(1)} %get-tuple-element.33), custom_call_target="InvertDiagBlocksLowerTriangular" | custom-call | tf_op jit(solution)/shard_map/jit(cholesky)/cholesky | solution.py:86
  293.6 0.3 constant_dynamic-update-slice_fusion.1
  293.9 0.3 convolution_subtract_fusion.2
  294.2 11.7 %cholesky.217 = f32[128,128]{1,0:T(8,128)S(1)} custom-call(f32[128,128]{1,0:T(8,128)S(1)} %cholesky.270), custom_call_target="Cholesky" | custom-call | tf_op jit(solution)/shard_map/jit(cholesky)/cholesky | solution.py:86
  306.0 10.2 %custom-call.31 = f32[1,128,128]{1,2,0:T(8,128)S(1)} custom-call(f32[1,128,128]{2,1,0:T(8,128)S(1)} %get-tuple-element.30), custom_call_target="InvertDiagBlocksLowerTriangular" | custom-call | tf_op jit(solution)/shard_map/jit(cholesky)/cholesky | solution.py:86
  316.4 0.4 convolution_subtract_fusion.3
  316.8 11.7 %cholesky.238 = f32[128,128]{1,0:T(8,128)S(1)} custom-call(f32[128,128]{1,0:T(8,128)S(1)} %cholesky.275), custom_call_target="Cholesky" | custom-call | tf_op jit(solution)/shard_map/jit(cholesky)/cholesky | solution.py:86
  328.6 0.6 compare_reduce_fusion.1
  329.2 9.8 %custom-call.32 = f32[1,128,128]{1,2,0:T(8,128)S(1)} custom-call(f32[1,128,128]{2,1,0:T(8,128)S(1)} %get-tuple-element.27), custom_call_target="InvertDiagBlocksLowerTriangular" | custom-call | tf_op jit(solution)/shard_map/jit(cholesky)/cholesky | solution.py:86
  339.3 0.4 convolution_subtract_fusion.4
  339.6 11.7 %cholesky.255 = f32[128,128]{1,0:T(8,128)S(1)} custom-call(f32[128,128]{1,0:T(8,128)S(1)} %convolution_subtract_fusion.4), custom_call_target="Cholesky" | custom-call | tf_op jit(solution)/shard_map/jit(cholesky)/cholesky | solution.py:86
  351.4 0.7 compare_reduce_fusion
  352.0 0.6 compare_reduce_fusion.2
  355.2 0.3 select_select_fusion
  355.6 8.0 %while.1 = (s32[]{:T(128)}, f32[512,512]{1,0:T(8,128)S(1)}, s32[4,2]{0,1:T(2,128)S(1)}, f32[4,128,128]{2,1,0:T(8,128)S(1)}, s32[]{:T(128)}) while((s32[]{:T(128)}, f32[512,512]{1,0:T(8,128)S(1)}, s32[4,2]{0,1:T(2,128)S(1)}, f32[4,128,128]{2,1,0:T(8,128)S(1)}, s32[]{:T(128)}) %tuple.32), condition=%wide.while_cond, body=%wide.while_body.sunk | while | flops 2 | bytes 131189 | solution.py:87
  355.7 0.5 fusion.58
  356.2 1.4 bitcast_dynamic-update-slice_fusion.2
  357.7 0.5 fusion.58
  358.2 1.4 bitcast_dynamic-update-slice_fusion.2
  359.7 0.5 fusion.58
  360.2 1.4 bitcast_dynamic-update-slice_fusion.2
  361.7 0.5 fusion.58
  362.2 1.4 bitcast_dynamic-update-slice_fusion.2
  363.6 39.3 %custom-call.33 = f32[4,128,128]{1,2,0:T(8,128)S(1)} custom-call(f32[4,128,128]{2,1,0:T(8,128)S(1)} %get-tuple-element.11), custom_call_target="InvertDiagBlocksLowerTriangular" | custom-call | tf_op jit(solution)/shard_map/triangular_solve | solution.py:87
  402.9 2.5 fusion.19
  405.4 3.1 convolution_subtract_fusion.1
  408.5 1.1 fusion.32
  409.6 4.6 convolution_subtract_fusion
  414.2 1.1 fusion.31
  415.3 7.2 fusion.8
  422.6 1.1 fusion.30
  423.7 27.9 %fusion = f32[1024,512]{1,0:T(8,128)} fusion(bf16[2048,1024]{1,0:T(8,128)(2,1)S(1)} %copy-done.8, bf16[2048,1024]{1,0:T(8,128)(2,1)S(1)} %copy-done.9, f32[2048,128]{0,1:T(8,128)S(1)} %fusion.30, f32[2048,128]{0,1:T(8,128)S(1)} %fusion.31, f32[2048,128]{0,1:T(8,128)S(1)} %fusion.32, f32[2048,128]{0,1:T(8,128)S(1)} %fusion.19), kind=kOutput, calls=%fused_computation.5 | convolution fusion | flops 12894339072 | bytes 14680064 | tf_op jit(solution)/shard_map/dot_general | solution.py:69
  451.6 6.2 all-to-all-start
  457.8 2.9 pad_maximum_fusion
  460.7 20.1 %all-to-all-done = f32[8,128,512]{2,1,0:T(8,128)} async-done(((f32[8,128,512]{2,1,0:T(8,128)}), f32[8,128,512]{2,1,0:T(8,128)}, u32[]{:S(2)}, u32[]{:S(2)}) %all-to-all-start) | async-done | bytes 2097184 | tf_op jit(solution)/shard_map/all_to_all | solution.py:25
  480.7 1.8 reduce_sum.27
  482.6 1.6 broadcast_in_dim.6
  484.1 5.7 all-to-all-start.1
  489.9 2.4 fusion.18
  492.3 2.3 copy.14
  494.7 21.2 %psum.51 = f32[512]{0:T(512)S(1)} all-reduce(f32[512]{0:T(512)S(1)} %multiply_reduce_fusion), channel_id=1, replica_groups=mesh['row_0'=4,'row_1'=2,'col_0'=4,'col_1'=2,'col_2'=2] {'row_0'}, use_global_device_ids=true, to_apply=%region_12.13 | all-reduce | flops 512 | bytes 4096 | tf_op jit(solution)/shard_map/psum | solution.py:30
  515.9 5.4 psum.52
  521.3 8.6 %psum.53 = f32[512]{0:T(512)S(1)} all-reduce(f32[512]{0:T(512)S(1)} %psum.52), channel_id=1, replica_groups=mesh['row_0'=4,'row_1'=2,'col_0'=4,'col_1'=2,'col_2'=2] {'col_0'}, use_global_device_ids=true, to_apply=%region_14.15 | all-reduce | flops 512 | bytes 4096 | tf_op jit(solution)/shard_map/psum | solution.py:30
  529.8 6.6 psum.54
  536.4 2.4 psum.55
  538.9 1.4 fusion.17
  540.4 1.7 copy.15
  542.1 1.6 broadcast_multiply_fusion
  543.7 106.3 %all-gather.5.cloned.1.call-done = bf16[16,1024,512]{2,1,0:T(8,128)(2,1)} async-done(((bf16[1,1024,512]{2,1,0:T(8,128)(2,1)}), bf16[16,1024,512]{2,1,0:T(8,128)(2,1)}) %all-gather.5.cloned.1.call-update) | async-done | bytes 16777232 | tf_op jit(solution)/shard_map/all_gather | solution.py:65
  649.9 1.7 dynamic-slice_bitcast_fusion.1
  651.6 39.3 %all-gather.3.cloned.1.call-done = bf16[1024,512]{0,1:T(8,128)(2,1)} async-done(((bf16[128,512]{0,1:T(8,128)(2,1)}), bf16[1024,512]{0,1:T(8,128)(2,1)}) %all-gather.3.cloned.1.call-update) | async-done | bytes 1048592 | tf_op jit(solution)/shard_map/all_gather | solution.py:61
  691.0 5.0 subtract_convert_fusion
  696.0 2.4 fusion.44
  698.4 8.6 %all-to-all-start.2 = ((f32[8,32,1024]{2,1,0:T(8,128)}), f32[8,32,1024]{2,1,0:T(8,128)}, u32[]{:S(2)}, u32[]{:S(2)}) async-start(f32[8,32,1024]{2,1,0:T(8,128)} %bitcast.17), calls=%async_computation.2 | async-start | bytes 2097152 | tf_op jit(solution)/shard_map/all_to_all | solution.py:25
  707.0 31.3 %subtract_convert_fusion.1 = bf16[2048,1024]{1,0:T(8,128)(2,1)} fusion(bf16[2048,1024]{1,0:T(8,128)(2,1)} %param.6, bf16[2048,1024]{1,0:T(8,128)(2,1)} %param.5, f32[1024,512]{1,0:T(8,128)} %bitcast.72, f32[2048,128]{0,1:T(8,128)} %copy-done.6, f32[2048,128]{0,1:T(8,128)} %copy-done.5, f32[2048,128]{0,1:T(8,128)} %copy-done.4, f32[2048,128]{0,1:T(8,128)S(1)} %fusion.19), kind=kOutput, calls=%fused_computation.3 | convolution fusion | flops 12900630528 | bytes 18874368 | tf_op jit(solution)/shard_map/dot_general | solution.py:75
  738.3 1.9 reduce_sum.29
  (55 shorter events, 1.4 us)
Async XLA Ops:
  7.2 1.6 copy-start
  7.2 166.3 %all-reduce.4.cloned.1.call-start = ((), (), s32[]{:S(2)}) async-start(), calls=%async_computation.4 | async-start | bytes 8388608 | tf_op jit(solution)/shard_map/psum | solution.py:84
  26.1 242.7 %all-reduce.6.cloned.1.call-start = ((), (), s32[]{:S(2)}) async-start(), calls=%async_computation.5 | async-start | bytes 2097152 | tf_op jit(solution)/shard_map/psum | solution.py:85
  363.6 39.3 %copy-start.7 = (f32[512,512]{1,0:T(8,128)}, f32[512,512]{1,0:T(8,128)S(1)}, u32[]{:S(2)}) copy-start(f32[512,512]{1,0:T(8,128)S(1)} %get-tuple-element.100) | copy-start | bytes 3145732
  402.9 6.6 copy-start.2
  409.6 48.2 %copy-start.4 = (f32[2048,128]{0,1:T(8,128)}, f32[2048,128]{0,1:T(8,128)S(1)}, u32[]{:S(2)}) copy-start(f32[2048,128]{0,1:T(8,128)S(1)} %fusion.32) | copy-start | bytes 3145732
  414.2 9.5 %copy-start.9 = (bf16[2048,1024]{1,0:T(8,128)(2,1)S(1)}, bf16[2048,1024]{1,0:T(8,128)(2,1)}, u32[]{:S(2)}) copy-start(bf16[2048,1024]{1,0:T(8,128)(2,1)} %param.5) | copy-start | bytes 12582916
  415.3 42.5 %copy-start.5 = (f32[2048,128]{0,1:T(8,128)}, f32[2048,128]{0,1:T(8,128)S(1)}, u32[]{:S(2)}) copy-start(f32[2048,128]{0,1:T(8,128)S(1)} %fusion.31) | copy-start | bytes 3145732
  415.3 8.4 %copy-start.8 = (bf16[2048,1024]{1,0:T(8,128)(2,1)S(1)}, bf16[2048,1024]{1,0:T(8,128)(2,1)}, u32[]{:S(2)}) copy-start(bf16[2048,1024]{1,0:T(8,128)(2,1)} %param.6) | copy-start | bytes 12582916
  423.7 27.9 %copy-start.6 = (f32[2048,128]{0,1:T(8,128)}, f32[2048,128]{0,1:T(8,128)S(1)}, u32[]{:S(2)}) copy-start(f32[2048,128]{0,1:T(8,128)S(1)} %fusion.30) | copy-start | bytes 3145732
  451.6 29.1 %all-to-all-start = ((f32[8,128,512]{2,1,0:T(8,128)}), f32[8,128,512]{2,1,0:T(8,128)}, u32[]{:S(2)}, u32[]{:S(2)}) async-start(f32[8,128,512]{2,1,0:T(8,128)} %bitcast.73), calls=%async_computation | async-start | bytes 4194304 | tf_op jit(solution)/shard_map/all_to_all | solution.py:25
  484.1 54.7 %all-to-all-start.1 = ((f32[8,128,512]{2,1,0:T(8,128)}), f32[8,128,512]{2,1,0:T(8,128)S(1)}, u32[]{:S(2)}, u32[]{:S(2)}) async-start(f32[8,128,512]{2,1,0:T(8,128)} %broadcast_in_dim.6), calls=%async_computation.1 | async-start | bytes 4194304 | tf_op jit(solution)/shard_map/all_to_all | solution.py:41
  489.9 50.5 %reduce-scatter.4.cloned.1.call-start = ((), (), s32[]{:S(2)}) async-start(), calls=%async_computation.8 | async-start | bytes 1179648
  494.6 155.3 %all-gather.5.cloned.1.call-start = ((), (), s32[]{:S(2)}) async-start(), calls=%async_computation.7 | async-start | bytes 17825792 | tf_op jit(solution)/shard_map/all_gather | solution.py:65
  538.9 4.8 copy-start.3
  540.3 150.7 %all-gather.3.cloned.1.call-start = ((), (), s32[]{:S(2)}) async-start(), calls=%async_computation.6 | async-start | bytes 1179648 | tf_op jit(solution)/shard_map/all_gather | solution.py:61
  691.0 5.0 copy-start.10
  696.0 2.4 copy-start.11
  698.4 39.9 %all-to-all-start.2 = ((f32[8,32,1024]{2,1,0:T(8,128)}), f32[8,32,1024]{2,1,0:T(8,128)}, u32[]{:S(2)}, u32[]{:S(2)}) async-start(f32[8,32,1024]{2,1,0:T(8,128)} %bitcast.17), calls=%async_computation.2 | async-start | bytes 2097152 | tf_op jit(solution)/shard_map/all_to_all | solution.py:25
  707.0 33.3 %copy-start.1 = (f32[1024,512]{1,0:T(8,128)S(1)}, f32[1024,512]{1,0:T(8,128)}, u32[]{:S(2)}) copy-start(f32[1024,512]{1,0:T(8,128)} %param.7) | copy-start | bytes 6291460
Sparse Core Ops, SparseCore 0:
  26.2 147.1 all-reduce.3
  185.2 83.6 all-reduce.5
  494.7 43.9 reduce-scatter.3
  541.5 108.3 all-gather.4
  651.9 38.9 all-gather.2
where the time goes:
time: 755 us; the launch traced here: 747 us
  waiting for transfers between devices  397 us (53%)
  other arithmetic  132 us (17%)
  matrix products  118 us (16%)
  blocking collectives  44.2 us (6%)
  starting transfers between devices  20.7 us (3%)
  local copies, waits for them, and re-layouts  18.4 us (2%)
  between operations  16.9 us (2%)
    psum x1, waiting for transfers between devices, per_device(): left_raw = lax.psum(partial_left, COL)  147 us
    all_gather x1, waiting for transfers between devices, from_root(): lax.all_gather(array, axis)  106 us
    psum x1, waiting for transfers between devices, per_device(): gram_matrix = lax.psum(contract_first(left_raw, left_raw, highest), ROW)  83.7 us
    another operation x14, other arithmetic, per_device(): factor = jnp.linalg.cholesky(gram_matrix)  78.7 us
    psum x5, blocking collectives, over_axes(): return functools.reduce(lax.psum, axes, array)  44.2 us
    another operation x4, other arithmetic, per_device(): lax.linalg.triangular_solve(factor, left_raw, left_side=False, lower=True...  42.5 us
    dot_general x2, matrix products, contract_first(): lax.dot_general(lhs, rhs, (((0,), (0,)), ((), ())), precision=highest, pr...  39.5 us
    all_gather x1, waiting for transfers between devices, spread(): lax.all_gather(own, axis, axis=0, tiled=True)[:len(lines)]  39.3 us
  transfers between devices with their start and end apart: 8, of which 5 were waited for; matrix products, arithmetic and copies ran while one was open for 6% of the time, Pallas kernels for 0%

commit v1 on v0

--- a/solution.py
+++ b/solution.py
@@ -81,7 +81,7 @@
     highest = lax.Precision.HIGHEST
     mixed = momentum.astype(jnp.float32) + gradient.astype(jnp.float32)
     partial_left = jnp.dot(mixed, right_prev, precision=highest, preferred_element_type=jnp.float32)
-    left_raw = lax.psum(partial_left, COL)
+    left_raw = lax.psum(lax.psum(partial_left, "col_0"), ("col_1", "col_2"))
     gram_matrix = lax.psum(contract_first(left_raw, left_raw, highest), ROW)
     factor = jnp.linalg.cholesky(gram_matrix)
     left_factor = lax.linalg.triangular_solve(

time: 755 us -> 791 us (1.048)
  waiting for transfers between devices: 397 us -> 433 us
    psum x1 -> x2, waiting for transfers between devices: 147 us -> 191 us  [per_device(): left_raw = lax.psum(lax.psum(partial_left, 'col_0'), ('col_1', 'col_2'))]
  transfers between devices with their start and end apart: 8 -> 9, of which waited for: 5 -> 6; matrix products, arithmetic and copies ran while one was open for 6% -> 6% of each run, Pallas kernels for 0% -> 0%
where the time goes in v1:
time: 791 us; the launch traced here: 783 us
  waiting for transfers between devices  433 us (55%)
  other arithmetic  132 us (17%)
  matrix products  118 us (15%)
  blocking collectives  44.1 us (6%)
  starting transfers between devices  20.7 us (3%)
  local copies, waits for them, and re-layouts  18.4 us (2%)
  between operations  17.2 us (2%)
    psum x2, waiting for transfers between devices, per_device(): left_raw = lax.psum(lax.psum(partial_left, 'col_0'), ('col_1', 'col_2'))  191 us
    all_gather x1, waiting for transfers between devices, from_root(): lax.all_gather(array, axis)  106 us
    another operation x14, other arithmetic, per_device(): factor = jnp.linalg.cholesky(gram_matrix)  78.7 us
    psum x1, waiting for transfers between devices, per_device(): gram_matrix = lax.psum(contract_first(left_raw, left_raw, highest), ROW)  75.9 us
    psum x5, blocking collectives, over_axes(): return functools.reduce(lax.psum, axes, array)  44.1 us
    another operation x4, other arithmetic, per_device(): lax.linalg.triangular_solve(factor, left_raw, left_side=False, lower=True...  42.5 us
    dot_general x2, matrix products, contract_first(): lax.dot_general(lhs, rhs, (((0,), (0,)), ((), ())), precision=highest, pr...  39.5 us
    all_gather x1, waiting for transfers between devices, spread(): lax.all_gather(own, axis, axis=0, tiled=True)[:len(lines)]  39.4 us
  transfers between devices with their start and end apart: 9, of which 6 were waited for; matrix products, arithmetic and copies ran while one was open for 6% of the time, Pallas kernels for 0%

profile of v1, /device:TPU:10, one launch (start us, length us, event | category | flops | bytes accessed | tf_op | source)
XLA Modules:
  0.0 783.0 jit_solution(7679584187423759304)
XLA Ops:
  7.2 1.5 copy-done
  8.8 17.3 %fusion.1 = f32[2048,512]{1,0:T(8,128)} fusion(f32[1024,512]{1,0:T(8,128)S(1)} %copy-done, bf16[2048,1024]{1,0:T(8,128)(2,1)} %param.6, bf16[2048,1024]{1,0:T(8,128)(2,1)} %param.5), kind=kOutput, calls=%fused_computation.6 | convolution fusion | flops 12891193344 | bytes 14680064 | tf_op jit(solution)/shard_map/dot_general | solution.py:83
  26.2 94.0 %all-reduce.5.cloned.1.call-done = f32[2048,512]{1,0:T(8,128)} async-done(((f32[2048,512]{1,0:T(8,128)}), f32[2048,512]{1,0:T(8,128)}) %all-reduce.5.cloned.1.call-update) | async-done | bytes 4194320 | tf_op jit(solution)/shard_map/psum | solution.py:84
  120.3 96.6 %all-reduce.7.cloned.1.call-done = f32[2048,512]{1,0:T(8,128)} async-done(((f32[2048,512]{1,0:T(8,128)}), f32[2048,512]{1,0:T(8,128)}) %all-reduce.7.cloned.1.call-update) | async-done | bytes 4194320 | tf_op jit(solution)/shard_map/psum | solution.py:84
  216.9 11.6 %fusion.43 = f32[512,512]{0,1:T(8,128)} fusion(f32[2048,512]{1,0:T(8,128)} %all-reduce.7.cloned.1.call-done), kind=kOutput, calls=%fused_computation.86 | convolution fusion | flops 6442450944 | bytes 5242880 | tf_op jit(solution)/shard_map/dot_general | solution.py:69
  228.5 75.9 %all-reduce.9.cloned.1.call-done = f32[512,512]{0,1:T(8,128)} async-done(((f32[512,512]{0,1:T(8,128)}), f32[512,512]{0,1:T(8,128)}) %all-reduce.9.cloned.1.call-update) | async-done | bytes 1048592 | tf_op jit(solution)/shard_map/psum | solution.py:85
  304.4 1.6 copy.12
  306.0 1.4 fusion.21
  307.5 11.7 %cholesky.104 = f32[128,128]{1,0:T(8,128)S(1)} custom-call(f32[128,128]{1,0:T(8,128)S(1)} %cholesky.266), custom_call_target="Cholesky" | custom-call | tf_op jit(solution)/shard_map/jit(cholesky)/cholesky | solution.py:86
  319.2 9.8 %custom-call.30 = f32[1,128,128]{1,2,0:T(8,128)S(1)} custom-call(f32[1,128,128]{2,1,0:T(8,128)S(1)} %get-tuple-element.33), custom_call_target="InvertDiagBlocksLowerTriangular" | custom-call | tf_op jit(solution)/shard_map/jit(cholesky)/cholesky | solution.py:86
  329.2 0.3 constant_dynamic-update-slice_fusion.1
  329.5 0.3 convolution_subtract_fusion.2
  329.8 11.7 %cholesky.217 = f32[128,128]{1,0:T(8,128)S(1)} custom-call(f32[128,128]{1,0:T(8,128)S(1)} %cholesky.270), custom_call_target="Cholesky" | custom-call | tf_op jit(solution)/shard_map/jit(cholesky)/cholesky | solution.py:86
  341.6 10.2 %custom-call.31 = f32[1,128,128]{1,2,0:T(8,128)S(1)} custom-call(f32[1,128,128]{2,1,0:T(8,128)S(1)} %get-tuple-element.30), custom_call_target="InvertDiagBlocksLowerTriangular" | custom-call | tf_op jit(solution)/shard_map/jit(cholesky)/cholesky | solution.py:86
  352.0 0.4 convolution_subtract_fusion.3
  352.4 11.7 %cholesky.238 = f32[128,128]{1,0:T(8,128)S(1)} custom-call(f32[128,128]{1,0:T(8,128)S(1)} %cholesky.275), custom_call_target="Cholesky" | custom-call | tf_op jit(solution)/shard_map/jit(cholesky)/cholesky | solution.py:86
  364.2 0.6 compare_reduce_fusion.1
  364.8 9.8 %custom-call.32 = f32[1,128,128]{1,2,0:T(8,128)S(1)} custom-call(f32[1,128,128]{2,1,0:T(8,128)S(1)} %get-tuple-element.27), custom_call_target="InvertDiagBlocksLowerTriangular" | custom-call | tf_op jit(solution)/shard_map/jit(cholesky)/cholesky | solution.py:86
  374.9 0.4 convolution_subtract_fusion.4
  375.2 11.7 %cholesky.255 = f32[128,128]{1,0:T(8,128)S(1)} custom-call(f32[128,128]{1,0:T(8,128)S(1)} %convolution_subtract_fusion.4), custom_call_target="Cholesky" | custom-call | tf_op jit(solution)/shard_map/jit(cholesky)/cholesky | solution.py:86
  387.0 0.7 compare_reduce_fusion
  387.6 0.6 compare_reduce_fusion.2
  391.2 8.0 %while.1 = (s32[]{:T(128)}, f32[512,512]{1,0:T(8,128)S(1)}, s32[4,2]{0,1:T(2,128)S(1)}, f32[4,128,128]{2,1,0:T(8,128)S(1)}, s32[]{:T(128)}) while((s32[]{:T(128)}, f32[512,512]{1,0:T(8,128)S(1)}, s32[4,2]{0,1:T(2,128)S(1)}, f32[4,128,128]{2,1,0:T(8,128)S(1)}, s32[]{:T(128)}) %tuple.32), condition=%wide.while_cond, body=%wide.while_body.sunk | while | flops 2 | bytes 131189 | solution.py:87
  391.3 0.5 fusion.58
  391.8 1.4 bitcast_dynamic-update-slice_fusion.2
  393.3 0.5 fusion.58
  393.8 1.4 bitcast_dynamic-update-slice_fusion.2
  395.3 0.5 fusion.58
  395.8 1.4 bitcast_dynamic-update-slice_fusion.2
  397.3 0.5 fusion.58
  397.8 1.4 bitcast_dynamic-update-slice_fusion.2
  399.2 39.3 %custom-call.33 = f32[4,128,128]{1,2,0:T(8,128)S(1)} custom-call(f32[4,128,128]{2,1,0:T(8,128)S(1)} %get-tuple-element.11), custom_call_target="InvertDiagBlocksLowerTriangular" | custom-call | tf_op jit(solution)/shard_map/triangular_solve | solution.py:87
  438.5 2.5 fusion.19
  441.0 3.1 convolution_subtract_fusion.1
  444.1 1.1 fusion.32
  445.2 4.6 convolution_subtract_fusion
  449.8 1.1 fusion.31
  450.9 7.2 fusion.8
  458.2 1.1 fusion.30
  459.3 27.9 %fusion = f32[1024,512]{1,0:T(8,128)} fusion(bf16[2048,1024]{1,0:T(8,128)(2,1)S(1)} %copy-done.8, bf16[2048,1024]{1,0:T(8,128)(2,1)S(1)} %copy-done.9, f32[2048,128]{0,1:T(8,128)S(1)} %fusion.30, f32[2048,128]{0,1:T(8,128)S(1)} %fusion.31, f32[2048,128]{0,1:T(8,128)S(1)} %fusion.32, f32[2048,128]{0,1:T(8,128)S(1)} %fusion.19), kind=kOutput, calls=%fused_computation.5 | convolution fusion | flops 12894339072 | bytes 14680064 | tf_op jit(solution)/shard_map/dot_general | solution.py:69
  487.2 6.2 all-to-all-start
  493.4 2.9 pad_maximum_fusion
  496.3 20.1 %all-to-all-done = f32[8,128,512]{2,1,0:T(8,128)} async-done(((f32[8,128,512]{2,1,0:T(8,128)}), f32[8,128,512]{2,1,0:T(8,128)}, u32[]{:S(2)}, u32[]{:S(2)}) %all-to-all-start) | async-done | bytes 2097184 | tf_op jit(solution)/shard_map/all_to_all | solution.py:25
  516.3 1.8 reduce_sum.27
  518.2 1.6 broadcast_in_dim.6
  519.7 5.7 all-to-all-start.1
  525.5 2.4 fusion.18
  527.9 2.3 copy.14
  530.3 21.2 %psum.59 = f32[512]{0:T(512)S(1)} all-reduce(f32[512]{0:T(512)S(1)} %multiply_reduce_fusion), channel_id=1, replica_groups=mesh['row_0'=4,'row_1'=2,'col_0'=4,'col_1'=2,'col_2'=2] {'row_0'}, use_global_device_ids=true, to_apply=%region_13.14 | all-reduce | flops 512 | bytes 4096 | tf_op jit(solution)/shard_map/psum | solution.py:30
  551.4 5.4 psum.60
  556.8 8.7 %psum.61 = f32[512]{0:T(512)S(1)} all-reduce(f32[512]{0:T(512)S(1)} %psum.60), channel_id=1, replica_groups=mesh['row_0'=4,'row_1'=2,'col_0'=4,'col_1'=2,'col_2'=2] {'col_0'}, use_global_device_ids=true, to_apply=%region_15.16 | all-reduce | flops 512 | bytes 4096 | tf_op jit(solution)/shard_map/psum | solution.py:30
  565.5 6.4 psum.62
  571.9 2.4 psum.63
  574.4 1.4 fusion.17
  575.9 1.7 copy.15
  577.6 1.6 broadcast_multiply_fusion
  579.2 106.5 %all-gather.5.cloned.1.call-done = bf16[16,1024,512]{2,1,0:T(8,128)(2,1)} async-done(((bf16[1,1024,512]{2,1,0:T(8,128)(2,1)}), bf16[16,1024,512]{2,1,0:T(8,128)(2,1)}) %all-gather.5.cloned.1.call-update) | async-done | bytes 16777232 | tf_op jit(solution)/shard_map/all_gather | solution.py:65
  685.7 1.7 dynamic-slice_bitcast_fusion.1
  687.3 39.4 %all-gather.3.cloned.1.call-done = bf16[1024,512]{0,1:T(8,128)(2,1)} async-done(((bf16[128,512]{0,1:T(8,128)(2,1)}), bf16[1024,512]{0,1:T(8,128)(2,1)}) %all-gather.3.cloned.1.call-update) | async-done | bytes 1048592 | tf_op jit(solution)/shard_map/all_gather | solution.py:61
  726.7 5.0 subtract_convert_fusion
  731.7 2.4 fusion.44
  734.1 8.6 %all-to-all-start.2 = ((f32[8,32,1024]{2,1,0:T(8,128)}), f32[8,32,1024]{2,1,0:T(8,128)}, u32[]{:S(2)}, u32[]{:S(2)}) async-start(f32[8,32,1024]{2,1,0:T(8,128)} %bitcast.17), calls=%async_computation.2 | async-start | bytes 2097152 | tf_op jit(solution)/shard_map/all_to_all | solution.py:25
  742.7 31.3 %subtract_convert_fusion.1 = bf16[2048,1024]{1,0:T(8,128)(2,1)} fusion(bf16[2048,1024]{1,0:T(8,128)(2,1)} %param.6, bf16[2048,1024]{1,0:T(8,128)(2,1)} %param.5, f32[1024,512]{1,0:T(8,128)} %bitcast.72, f32[2048,128]{0,1:T(8,128)} %copy-done.6, f32[2048,128]{0,1:T(8,128)} %copy-done.5, f32[2048,128]{0,1:T(8,128)} %copy-done.4, f32[2048,128]{0,1:T(8,128)S(1)} %fusion.19), kind=kOutput, calls=%fused_computation.3 | convolution fusion | flops 12900630528 | bytes 18874368 | tf_op jit(solution)/shard_map/dot_general | solution.py:75
  774.1 1.9 reduce_sum.29
  (58 shorter events, 1.8 us)
Async XLA Ops:
  7.2 1.6 copy-start
  7.2 113.0 %all-reduce.5.cloned.1.call-start = ((), (), s32[]{:S(2)}) async-start(), calls=%async_computation.4 | async-start | bytes 8388608 | tf_op jit(solution)/shard_map/psum | solution.py:84
  26.1 190.8 %all-reduce.7.cloned.1.call-start = ((), (), s32[]{:S(2)}) async-start(), calls=%async_computation.5 | async-start | bytes 8388608 | tf_op jit(solution)/shard_map/psum | solution.py:84
  120.2 184.2 %all-reduce.9.cloned.1.call-start = ((), (), s32[]{:S(2)}) async-start(), calls=%async_computation.6 | async-start | bytes 2097152 | tf_op jit(solution)/shard_map/psum | solution.py:85
  399.2 39.3 %copy-start.7 = (f32[512,512]{1,0:T(8,128)}, f32[512,512]{1,0:T(8,128)S(1)}, u32[]{:S(2)}) copy-start(f32[512,512]{1,0:T(8,128)S(1)} %get-tuple-element.104) | copy-start | bytes 3145732
  438.5 6.6 copy-start.2
  445.2 48.2 %copy-start.4 = (f32[2048,128]{0,1:T(8,128)}, f32[2048,128]{0,1:T(8,128)S(1)}, u32[]{:S(2)}) copy-start(f32[2048,128]{0,1:T(8,128)S(1)} %fusion.32) | copy-start | bytes 3145732
  449.8 9.5 %copy-start.9 = (bf16[2048,1024]{1,0:T(8,128)(2,1)S(1)}, bf16[2048,1024]{1,0:T(8,128)(2,1)}, u32[]{:S(2)}) copy-start(bf16[2048,1024]{1,0:T(8,128)(2,1)} %param.5) | copy-start | bytes 12582916
  450.9 42.5 %copy-start.5 = (f32[2048,128]{0,1:T(8,128)}, f32[2048,128]{0,1:T(8,128)S(1)}, u32[]{:S(2)}) copy-start(f32[2048,128]{0,1:T(8,128)S(1)} %fusion.31) | copy-start | bytes 3145732
  450.9 8.4 %copy-start.8 = (bf16[2048,1024]{1,0:T(8,128)(2,1)S(1)}, bf16[2048,1024]{1,0:T(8,128)(2,1)}, u32[]{:S(2)}) copy-start(bf16[2048,1024]{1,0:T(8,128)(2,1)} %param.6) | copy-start | bytes 12582916
  459.3 27.9 %copy-start.6 = (f32[2048,128]{0,1:T(8,128)}, f32[2048,128]{0,1:T(8,128)S(1)}, u32[]{:S(2)}) copy-start(f32[2048,128]{0,1:T(8,128)S(1)} %fusion.30) | copy-start | bytes 3145732
  487.2 29.1 %all-to-all-start = ((f32[8,128,512]{2,1,0:T(8,128)}), f32[8,128,512]{2,1,0:T(8,128)}, u32[]{:S(2)}, u32[]{:S(2)}) async-start(f32[8,128,512]{2,1,0:T(8,128)} %bitcast.73), calls=%async_computation | async-start | bytes 4194304 | tf_op jit(solution)/shard_map/all_to_all | solution.py:25
  519.7 54.6 %all-to-all-start.1 = ((f32[8,128,512]{2,1,0:T(8,128)}), f32[8,128,512]{2,1,0:T(8,128)S(1)}, u32[]{:S(2)}, u32[]{:S(2)}) async-start(f32[8,128,512]{2,1,0:T(8,128)} %broadcast_in_dim.6), calls=%async_computation.1 | async-start | bytes 4194304 | tf_op jit(solution)/shard_map/all_to_all | solution.py:41
  525.5 50.4 %reduce-scatter.4.cloned.1.call-start = ((), (), s32[]{:S(2)}) async-start(), calls=%async_computation.9 | async-start | bytes 1179648
  530.2 155.5 %all-gather.5.cloned.1.call-start = ((), (), s32[]{:S(2)}) async-start(), calls=%async_computation.8 | async-start | bytes 17825792 | tf_op jit(solution)/shard_map/all_gather | solution.py:65
  574.4 4.8 copy-start.3
  575.8 150.9 %all-gather.3.cloned.1.call-start = ((), (), s32[]{:S(2)}) async-start(), calls=%async_computation.7 | async-start | bytes 1179648 | tf_op jit(solution)/shard_map/all_gather | solution.py:61
  726.7 5.0 copy-start.10
  731.7 2.4 copy-start.11
  734.1 39.9 %all-to-all-start.2 = ((f32[8,32,1024]{2,1,0:T(8,128)}), f32[8,32,1024]{2,1,0:T(8,128)}, u32[]{:S(2)}, u32[]{:S(2)}) async-start(f32[8,32,1024]{2,1,0:T(8,128)} %bitcast.17), calls=%async_computation.2 | async-start | bytes 2097152 | tf_op jit(solution)/shard_map/all_to_all | solution.py:25
  742.7 33.3 %copy-start.1 = (f32[1024,512]{1,0:T(8,128)S(1)}, f32[1024,512]{1,0:T(8,128)}, u32[]{:S(2)}) copy-start(f32[1024,512]{1,0:T(8,128)} %param.7) | copy-start | bytes 6291460
Sparse Core Ops, SparseCore 0:
  26.2 93.9 all-reduce.4
  122.9 93.9 all-reduce.6
  228.6 75.7 all-reduce.8
  530.3 43.7 reduce-scatter.3
  576.9 108.7 all-gather.4
  687.7 38.9 all-gather.2
